TPU v7x, 128 devices: a whole 4x4x4 slice. The times are simulated.
128 devices in a mesh: slot: 16 (over y, z), head: 2 (over x_lo), conv: 4 (over x_hi, core).
Axes of the slice: x: 4 (x_hi: 2, x_lo: 2; x = x_hi * 2 + x_lo), y: 4, z: 4, core: 2. Of those that a mesh axis runs over, the one named last changes fastest.
Arguments:
- queries: bfloat16 [1024, 64, 128], P(('conv', 'slot'), 'head'), may hold values from -96 to 96
- out_grad: bfloat16 [1024, 64, 128], P(('conv', 'slot'), 'head'), may hold values from -768 to 768
- row_positions: int32 [1024], P('conv'), may hold values from 0 to 8191
- slot_offsets: int32 [16384], P('slot'), may hold values from 0 to 16382, as said below
- cache: float32 [2, 16384, 4, 128], P(None, 'slot', 'head'), may hold values from -12 to 12
- first_moment: float32 [2, 16384, 4, 128], P(None, 'slot', 'head'), may hold values from -6 to 6
- second_moment: float32 [2, 16384, 4, 128], P(None, 'slot', 'head'), may hold values from 0.01 to 1000
Outputs:
- new_cache: float32 [2, 16384, 4, 128], P(None, 'slot', 'head')
- new_first_moment: float32 [2, 16384, 4, 128], P(None, 'slot', 'head')
- new_second_moment: float32 [2, 16384, 4, 128], P(None, 'slot', 'head')
- query_grad: float32 [1024, 64, 128], P(('conv', 'slot'), 'head')
Inputs may be any that keep to these rules, and one draw needn't show every extreme that they name: `slot_offsets`: never falls from one slot to the next; its first two entries are 0.
All inputs are finite; a program needn't handle non-finite values.
Results may differ from a plain program's by a relative error of at most 0.012.
The roundings to bfloat16 on the way count: a program that leaves them out, or rounds other values in their place, can miss the bound.
Values may be sent and summed in bfloat16 or wider, within the bound.
A program may use at most 128 MiB of HBM per device.

v0:
```python
import math
import jax
import jax.numpy as jnp
from jax import lax
from jax.sharding import PartitionSpec as P

STEP = 20
learn_rate = 0.01
beta_one = 0.9
beta_two = 0.95
adam_eps = 1e-08
masked_score = -1e30


def merged(x, axis, combine):
    everything = jax.tree.map(lambda part: lax.all_gather(part, axis), x)
    leading = jax.tree.map(lambda part: part[0], everything)

    def lap(k, so_far):
        return combine(so_far, jax.tree.map(lambda part: part[k], everything))

    return lax.fori_loop(1, lax.axis_size(axis), lap, leading)


def merge_pairs(earlier, later):
    largest = jnp.maximum(earlier[0], later[0])
    return (
        largest,
        earlier[1] * jnp.exp(earlier[0] - largest) + later[1] * jnp.exp(later[0] - largest),
    )


def local(queries, out_grad, row_positions, slot_offsets, cache, first_moment, second_moment):
    query_all, grad_all = (
        lax.all_gather(queries, "slot", axis=0, tiled=True),
        lax.all_gather(out_grad, "slot", axis=0, tiled=True),
    )
    total_rows, head_count, head_width = query_all.shape
    kv_count = cache.shape[2]
    group_heads = head_count // kv_count
    score_scale = 1.0 / math.sqrt(head_width)
    block_rows = min(64, total_rows)
    block_count = total_rows // block_rows
    key_half = cache[0].astype(jnp.bfloat16)
    value_half = cache[1].astype(jnp.bfloat16)
    query_blocks = query_all.reshape(block_count, block_rows, kv_count, group_heads, head_width)
    grad_blocks = grad_all.reshape(block_count, block_rows, kv_count, group_heads, head_width)
    visible_all = (slot_offsets[None, :] <= row_positions[:, None]).reshape(
        block_count, block_rows, -1
    )

    def masked_scores(query_block, visible):
        raw_score = (
            jnp.einsum("rkgd,skd->rkgs", query_block, key_half, preferred_element_type=jnp.float32)
            * score_scale
        )
        return jnp.where(visible[:, None, None, :], raw_score, masked_score)

    def weights_from(scores, visible, offset):
        return jnp.where(visible[:, None, None, :], jnp.exp(scores - offset[..., None]), 0.0)

    def gradient_products(grad_block):
        return jnp.einsum(
            "rkgd,skd->rkgs", grad_block, value_half, preferred_element_type=jnp.float32
        )

    def max_pass(inputs):
        query_block, visible = inputs
        scores = masked_scores(query_block, visible)
        largest = jnp.max(scores, axis=-1)
        return (largest, jnp.sum(weights_from(scores, visible, largest), axis=-1))

    largest, denominator = lax.map(max_pass, (query_blocks, visible_all))
    largest, denominator = merged((largest, denominator), "slot", merge_pairs)
    log_total = largest + jnp.log(denominator)

    def product_pass(inputs):
        query_block, grad_block, visible, block_total = inputs
        probability = weights_from(masked_scores(query_block, visible), visible, block_total)
        return jnp.sum(probability * gradient_products(grad_block), axis=-1)

    partial_sum = lax.map(product_pass, (query_blocks, grad_blocks, visible_all, log_total))
    row_sum = lax.psum(partial_sum, "slot")

    def last_pass(running, inputs):
        key_grad, value_grad = running
        query_block, grad_block, visible, block_total, block_sum = inputs
        probability = weights_from(masked_scores(query_block, visible), visible, block_total)
        prob_grad = gradient_products(grad_block)
        score_grad = (probability * (prob_grad - block_sum[..., None])).astype(jnp.bfloat16)
        prob_half = probability.astype(jnp.bfloat16)
        value_grad = value_grad + jnp.einsum(
            "rkgs,rkgd->skd", prob_half, grad_block, preferred_element_type=jnp.float32
        )
        key_grad = (
            key_grad
            + jnp.einsum(
                "rkgs,rkgd->skd", score_grad, query_block, preferred_element_type=jnp.float32
            )
            * score_scale
        )
        query_part = (
            jnp.einsum("rkgs,skd->rkgd", score_grad, key_half, preferred_element_type=jnp.float32)
            * score_scale
        )
        return ((key_grad, value_grad), query_part)

    empty_grad = jnp.zeros(key_half.shape, jnp.float32)
    (key_grad, value_grad), query_parts = lax.scan(
        last_pass,
        (empty_grad, empty_grad),
        (query_blocks, grad_blocks, visible_all, log_total, row_sum),
    )
    query_terms = query_parts.reshape(total_rows, head_count, head_width)
    summed = lax.psum(query_terms, "slot")
    own_rows = queries.shape[0]
    query_grad = lax.dynamic_slice_in_dim(summed, lax.axis_index("slot") * own_rows, own_rows, 0)
    key_total, value_total = lax.psum((key_grad, value_grad), "conv")
    slot_grad = jnp.stack([key_total, value_total])
    new_first = beta_one * first_moment + (1.0 - beta_one) * slot_grad
    new_second = beta_two * second_moment + (1.0 - beta_two) * slot_grad * slot_grad
    first_fix = 1.0 - beta_one**STEP
    second_fix = 1.0 - beta_two**STEP
    new_cache = cache - learn_rate * (new_first / first_fix) / (
        jnp.sqrt(new_second / second_fix) + adam_eps
    )
    return (new_cache, new_first, new_second, query_grad)


def solution(mesh):
    in_specs = (
        P(("conv", "slot"), "head", None),
        P(("conv", "slot"), "head", None),
        P("conv"),
        P("slot"),
        P(None, "slot", "head", None),
        P(None, "slot", "head", None),
        P(None, "slot", "head", None),
    )
    out_specs = (
        P(None, "slot", "head", None),
        P(None, "slot", "head", None),
        P(None, "slot", "head", None),
        P(("conv", "slot"), "head", None),
    )
    return jax.shard_map(local, mesh=mesh, in_specs=in_specs, out_specs=out_specs, check_vma=False)
```

profile of v0, /device:TPU:1, one launch (start us, length us, event | category | flops | bytes accessed | tf_op | source)
XLA Modules:
  0.0 525.3 jit_solution(10511550598650439508)
XLA Ops:
  13.1 43.8 %all-gather.5.cloned.1.call-done = bf16[256,32,128]{2,1,0:T(8,128)(2,1)} async-done(((bf16[16,32,128]{2,1,0:T(8,128)(2,1)}), bf16[256,32,128]{2,1,0:T(8,128)(2,1)}) %all-gather.5.cloned.1.call-update) | async-done | bytes 2097168 | tf_op jit(solution)/shard_map/all_gather | solution.py:35
  56.9 3.3 copy.50
  60.1 43.2 %all-gather.7.cloned.1.call-done = bf16[256,32,128]{2,1,0:T(8,128)(2,1)} async-done(((bf16[16,32,128]{2,1,0:T(8,128)(2,1)}), bf16[256,32,128]{2,1,0:T(8,128)(2,1)}) %all-gather.7.cloned.1.call-update) | async-done | bytes 2097168 | tf_op jit(solution)/shard_map/all_gather | solution.py:36
  103.3 3.3 copy.51
  106.6 23.2 %while.54 = (s32[]{:T(128)}, f32[4,64,2,16]{1,3,2,0:T(8,128)S(1)}, f32[4,64,2,16]{1,3,2,0:T(8,128)S(1)}, pred[4,64,1024]{2,1,0:T(8,128)(4,1)S(1)}, bf16[4,64,2,1...) while((s32[]{:T(128)}, f32[4,64,2,16]{1,3,2,0:T(8,128)S(1)}, ...), condition=%wide.region_3.4_spmd, body=%wide.region_0.3_spmd.sunk | while | flops 553644032 | bytes 18210912 | solution.py:73
  121.0 2.8 fusion.87
  126.8 2.8 fusion.87
  129.8 19.1 %all-gather.1 = f32[64,64,2,16]{1,3,2,0:T(8,128)S(1)} all-gather(f32[4,64,2,16]{1,3,2,0:T(8,128)S(1)} %get-tuple-element.272), channel_id=3, replica_groups=mesh['slot'=16,'head'=2,'conv'=4] {'slot'}, dimensions={0}, use_global_device_ids=true | all-gather | bytes 557056 | tf_op jit(solution)/shard_map/all_gather | solution.py:16
  148.9 17.4 %all-gather = f32[64,64,2,16]{1,3,2,0:T(8,128)S(1)} all-gather(f32[4,64,2,16]{1,3,2,0:T(8,128)S(1)} %get-tuple-element.271), channel_id=2, replica_groups=mesh['slot'=16,'head'=2,'conv'=4] {'slot'}, dimensions={0}, use_global_device_ids=true | all-gather | bytes 557056 | tf_op jit(solution)/shard_map/all_gather | solution.py:16
  167.2 13.9 %while.55 = (s32[]{:T(128)}, f32[4,64,2,16]{1,3,2,0:T(8,128)S(1)}, f32[4,64,2,16]{1,3,2,0:T(8,128)S(1)}, f32[16,4,64,2,16]{2,4,3,1,0:T(8,128)}, f32[16,4,64,2,16...) while((s32[]{:T(128)}, f32[4,64,2,16]{1,3,2,0:T(8,128)S(1)}, f32[4,64,2,16]{1,3,2,0:T(8,128)S(1)}, ...), condition=%wide.region_5.6_spmd, body=%wide.region_4.5_spmd.sunk | while | flops 49157 | bytes 196731 | solution.py:22
  181.5 31.2 %while.56 = (s32[]{:T(128)}, f32[4,64,2,16]{3,1,2,0:T(8,128)}, pred[4,64,1024]{2,1,0:T(8,128)(4,1)S(1)}, bf16[4,64,2,16,128]{4,3,1,2,0:T(8,128)(2,1)}, bf16[1024...) while((s32[]{:T(128)}, f32[4,64,2,16]{3,1,2,0:T(8,128)}, ...), condition=%wide.region_8.9_spmd, body=%wide.region_6.8_spmd.sunk | while | flops 1086322688 | bytes 21397652 | solution.py:82
  183.9 4.7 fusion.94
  191.7 4.7 fusion.94
  199.5 4.7 fusion.94
  207.3 4.7 fusion.94
  212.7 61.1 %psum.28 = f32[4,64,2,16]{3,1,2,0:T(8,128)S(1)} all-reduce(f32[4,64,2,16]{3,1,2,0:T(8,128)} %get-tuple-element.275), channel_id=1, replica_groups=mesh['slot'=16,'head'=2,'conv'=4] {'slot'}, use_global_device_ids=true, to_apply=%region_9.10 | all-reduce | flops 8192 | bytes 65536 | tf_op jit(solution)/shard_map/psum | solution.py:83
  273.8 52.7 %while.57 = (s32[]{:T(128)}, f32[1024,2,128]{0,2,1:T(8,128)S(1)}, f32[1024,2,128]{0,2,1:T(8,128)S(1)}, f32[4,64,2,16,128]{4,3,2,1,0:T(8,128)}, bf16[4,64,2,16,12...) while((s32[]{:T(128)}, f32[1024,2,128]{0,2,1:T(8,128)S(1)}, ...), condition=%wide.region_11.12_spmd.clone, body=%wide.region_10.11_spmd.clone.sunk | while | flops 2711093248 | bytes 59867360 | solution.py:109
  279.1 3.5 fusion.106
  292.2 3.5 fusion.106
  305.4 3.5 fusion.106
  318.6 3.5 fusion.106
  329.7 81.8 %all-reduce.6.cloned.1.call-done = (f32[1,1024,2,128]{3,2,1,0:T(2,128)}, f32[1,1024,2,128]{3,2,1,0:T(2,128)}) async-done(((f32[1,1024,2,128]{3,2,1,0:T(2,128)}, f32[1,1024,2,128]{3,2,1,0:T(2,128)}), (f32[1,1024,2,128]{3,2,1,0:T(2,128)}, f32[1,1024,2,128]{3,2,1,0:T(2,128)})) %all-reduce.6.cloned.1.call-update) | async-done | bytes 2097168 | tf_op jit(solution)/shard_map/psum | solution.py:118
  414.5 8.0 %divide_subtract_fusion = (f32[2,1024,2,128]{3,2,1,0:T(2,128)}, f32[2,1024,2,128]{3,2,1,0:T(2,128)}, f32[2,1024,2,128]{3,2,1,0:T(2,128)}) fusion(f32[2,1024,2,128]{3,2,1,0:T(2,128)S(1)} %copy-done, f32[2,1024,2,128]{3,2,1,0:T(2,128)S(1)} %constant_dynamic-update-slice_fusion.2, f32[2,1024,2,128]{3,2,1,0:T(2,128)S(1)} %copy-done.1, ...), kind=kLoop, calls=%fused_computation.80 | loop fusion | flops 6291456 | bytes 14680064 | tf_op jit(solution)/shard_map/sub | solution.py:124
  422.5 94.6 %all-reduce.4.cloned.1.call-done = f32[256,32,128]{2,1,0:T(8,128)} async-done(((f32[256,32,128]{2,1,0:T(8,128)}), f32[256,32,128]{2,1,0:T(8,128)}) %all-reduce.4.cloned.1.call-update) | async-done | bytes 4194320 | tf_op jit(solution)/shard_map/psum | solution.py:115
  (143 shorter events, 96.5 us)
Async XLA Ops:
  7.2 49.7 %all-gather.5.cloned.1.call-start = ((), (), s32[]{:S(2)}) async-start(), calls=%async_computation | async-start | bytes 2228224 | tf_op jit(solution)/shard_map/all_gather | solution.py:35
  7.9 95.4 %all-gather.7.cloned.1.call-start = ((), (), s32[]{:S(2)}) async-start(), calls=%async_computation.1 | async-start | bytes 2228224 | tf_op jit(solution)/shard_map/all_gather | solution.py:36
  8.6 402.9 %all-reduce.6.cloned.1.call-start = ((), (), s32[]{:S(2)}) async-start(), calls=%async_computation.3 | async-start | bytes 4194304 | tf_op jit(solution)/shard_map/psum | solution.py:118
  166.2 1.0 copy-start.4
  181.4 92.4 %copy-start.5 = (f32[1024,2,128]{0,2,1:T(8,128)S(1)}, f32[1024,2,128]{0,2,1:T(8,128)}, u32[]{:S(2)}) copy-start(f32[1024,2,128]{0,2,1:T(8,128)} %custom-call.1) | copy-start | bytes 3145732
  181.5 2.4 copy-start.6
  189.3 2.4 copy-start.6
  197.1 2.4 copy-start.6
  204.9 2.4 copy-start.6
  273.9 2.5 copy-start.3
  276.4 2.7 copy-start.7
  287.1 2.5 copy-start.3
  289.5 2.7 copy-start.7
  300.3 2.5 copy-start.3
  302.7 2.7 copy-start.7
  313.4 2.5 copy-start.3
  315.9 2.7 copy-start.7
  329.2 187.9 %all-reduce.4.cloned.1.call-start = ((), (), s32[]{:S(2)}) async-start(), calls=%async_computation.2 | async-start | bytes 8388608 | tf_op jit(solution)/shard_map/psum | solution.py:115
  329.2 85.2 %copy-start = (f32[2,1024,2,128]{3,2,1,0:T(2,128)S(1)}, f32[2,1024,2,128]{3,2,1,0:T(2,128)}, u32[]{:S(2)}) copy-start(f32[2,1024,2,128]{3,2,1,0:T(2,128)} %param.19) | copy-start | bytes 6291460
  411.5 3.0 copy-start.1
  411.5 3.0 copy-start.2
Sparse Core Ops, SparseCore 0:
  10.1 46.6 all-gather.4
  59.0 44.2 all-gather.6
  329.3 82.1 all-reduce.5
  414.7 102.2 all-reduce.3
where the time goes:
time: 527 us; the launch traced here: 525 us
  waiting for transfers between devices  265 us (50%)
  blocking collectives  97.6 us (19%)
  matrix products  87.3 us (17%)
  other arithmetic  33.9 us (6%)
  local copies, waits for them, and re-layouts  26.4 us (5%)
  between operations  13.9 us (3%)
    psum x1, waiting for transfers between devices, local(): summed = lax.psum(query_terms, 'slot')  94.6 us
    psum x1, waiting for transfers between devices, local(): key_total, value_total = lax.psum((key_grad, value_grad), 'conv')  81.8 us
    psum x1, blocking collectives, local(): row_sum = lax.psum(partial_sum, 'slot')  61.1 us
    all_gather x1, waiting for transfers between devices, local(): lax.all_gather(queries, 'slot', axis=0, tiled=True)  43.8 us
    all_gather x1, waiting for transfers between devices, local(): lax.all_gather(out_grad, 'slot', axis=0, tiled=True)  43.2 us
    all_gather x2, blocking collectives, merged(): everything = jax.tree.map(lambda part: lax.all_gather(part, axis), x)  36.5 us
    dot_general x8, matrix products, gradient_products(): jnp.einsum('rkgd,skd->rkgs', grad_block, value_half, preferred_element_ty...  32.8 us
    dot_general x12, matrix products, masked_scores(): jnp.einsum('rkgd,skd->rkgs', query_block, key_half, preferred_element_typ...  30.3 us
  transfers between devices with their start and end apart: 4, of which 4 were waited for; matrix products, arithmetic and copies ran while one was open for 4% of the time, Pallas kernels for 0%

commit v1 on v0

--- a/solution.py
+++ b/solution.py
@@ -80,7 +80,8 @@
         return jnp.sum(probability * gradient_products(grad_block), axis=-1)
 
     partial_sum = lax.map(product_pass, (query_blocks, grad_blocks, visible_all, log_total))
-    row_sum = lax.psum(partial_sum, "slot")
+    parts = lax.all_gather(partial_sum, "slot")
+    row_sum = jnp.sum(parts, axis=0)
 
     def last_pass(running, inputs):
         key_grad, value_grad = running

time: 527 us -> 479 us (0.909)
  blocking collectives: 97.6 us -> 55.6 us
  waiting for transfers between devices: 265 us -> 257 us
    psum x1 -> x0, blocking collectives: 61.1 us -> none  [local(): row_sum = lax.psum(partial_sum, 'slot')]
    all_gather x0 -> x1, blocking collectives: none -> 19 us  [local(): parts = lax.all_gather(partial_sum, 'slot')]
    psum x1, waiting for transfers between devices: 81.8 us -> 73.8 us  [local(): key_total, value_total = lax.psum((key_grad, value_grad), 'conv')]
where the time goes in v1:
time: 479 us; the launch traced here: 477 us
  waiting for transfers between devices  257 us (54%)
  matrix products  86.9 us (18%)
  blocking collectives  55.6 us (12%)
  other arithmetic  35.8 us (7%)
  local copies, waits for them, and re-layouts  27.1 us (6%)
  between operations  13.9 us (3%)
    psum x1, waiting for transfers between devices, local(): summed = lax.psum(query_terms, 'slot')  93.1 us
    psum x1, waiting for transfers between devices, local(): key_total, value_total = lax.psum((key_grad, value_grad), 'conv')  73.8 us
    all_gather x1, waiting for transfers between devices, local(): lax.all_gather(queries, 'slot', axis=0, tiled=True)  44.6 us
    all_gather x1, waiting for transfers between devices, local(): lax.all_gather(out_grad, 'slot', axis=0, tiled=True)  43.2 us
    all_gather x2, blocking collectives, merged(): everything = jax.tree.map(lambda part: lax.all_gather(part, axis), x)  36.6 us
    dot_general x8, matrix products, gradient_products(): jnp.einsum('rkgd,skd->rkgs', grad_block, value_half, preferred_element_ty...  32.7 us
    dot_general x12, matrix products, masked_scores(): jnp.einsum('rkgd,skd->rkgs', query_block, key_half, preferred_element_typ...  30.1 us
    all_gather x1, blocking collectives, local(): parts = lax.all_gather(partial_sum, 'slot')  19 us
  transfers between devices with their start and end apart: 4, of which 4 were waited for; matrix products, arithmetic and copies ran while one was open for 4% of the time, Pallas kernels for 0%

profile of v1, /device:TPU:1, one launch (start us, length us, event | category | flops | bytes accessed | tf_op | source)
XLA Modules:
  0.0 477.0 jit_solution(2266693866155780145)
XLA Ops:
  12.2 44.6 %all-gather.6.cloned.1.call-done = bf16[256,32,128]{2,1,0:T(8,128)(2,1)} async-done(((bf16[16,32,128]{2,1,0:T(8,128)(2,1)}), bf16[256,32,128]{2,1,0:T(8,128)(2,1)}) %all-gather.6.cloned.1.call-update) | async-done | bytes 2097168 | tf_op jit(solution)/shard_map/all_gather | solution.py:35
  56.9 3.3 copy.49
  60.1 43.2 %all-gather.8.cloned.1.call-done = bf16[256,32,128]{2,1,0:T(8,128)(2,1)} async-done(((bf16[16,32,128]{2,1,0:T(8,128)(2,1)}), bf16[256,32,128]{2,1,0:T(8,128)(2,1)}) %all-gather.8.cloned.1.call-update) | async-done | bytes 2097168 | tf_op jit(solution)/shard_map/all_gather | solution.py:36
  103.3 3.3 copy.50
  106.6 23.2 %while.54 = (s32[]{:T(128)}, f32[4,64,2,16]{1,3,2,0:T(8,128)S(1)}, f32[4,64,2,16]{1,3,2,0:T(8,128)S(1)}, pred[4,64,1024]{2,1,0:T(8,128)(4,1)S(1)}, bf16[4,64,2,1...) while((s32[]{:T(128)}, f32[4,64,2,16]{1,3,2,0:T(8,128)S(1)}, ...), condition=%wide.region_3.4_spmd, body=%wide.region_0.3_spmd.sunk | while | flops 553644032 | bytes 18210912 | solution.py:73
  115.2 2.8 fusion.87
  121.0 2.8 fusion.87
  131.1 19.1 %all-gather.1 = f32[64,64,2,16]{1,3,2,0:T(8,128)S(1)} all-gather(f32[4,64,2,16]{1,3,2,0:T(8,128)} %copy-done.6), channel_id=3, replica_groups=mesh['slot'=16,'head'=2,'conv'=4] {'slot'}, dimensions={0}, use_global_device_ids=true | all-gather | bytes 557056 | tf_op jit(solution)/shard_map/all_gather | solution.py:16
  150.2 17.5 %all-gather = f32[64,64,2,16]{1,3,2,0:T(8,128)S(1)} all-gather(f32[4,64,2,16]{1,3,2,0:T(8,128)} %copy-done.7), channel_id=2, replica_groups=mesh['slot'=16,'head'=2,'conv'=4] {'slot'}, dimensions={0}, use_global_device_ids=true | all-gather | bytes 557056 | tf_op jit(solution)/shard_map/all_gather | solution.py:16
  168.6 13.9 %while.55 = (s32[]{:T(128)}, f32[4,64,2,16]{1,3,2,0:T(8,128)S(1)}, f32[4,64,2,16]{1,3,2,0:T(8,128)S(1)}, f32[16,4,64,2,16]{2,4,3,1,0:T(8,128)}, f32[16,4,64,2,16...) while((s32[]{:T(128)}, f32[4,64,2,16]{1,3,2,0:T(8,128)S(1)}, f32[4,64,2,16]{1,3,2,0:T(8,128)S(1)}, ...), condition=%wide.region_5.6_spmd, body=%wide.region_4.5_spmd.sunk | while | flops 49157 | bytes 196731 | solution.py:22
  182.9 28.5 %while.56 = (s32[]{:T(128)}, f32[4,64,2,16]{1,3,2,0:T(8,128)S(1)}, pred[4,64,1024]{2,1,0:T(8,128)(4,1)S(1)}, bf16[4,64,2,16,128]{4,3,1,2,0:T(8,128)(2,1)}, bf16[...) while((s32[]{:T(128)}, f32[4,64,2,16]{1,3,2,0:T(8,128)S(1)}, ...), condition=%wide.region_8.9_spmd, body=%wide.region_6.8_spmd.sunk | while | flops 1086322688 | bytes 19275896 | solution.py:82
  185.2 4.7 fusion.94
  192.4 4.7 fusion.94
  199.5 4.7 fusion.94
  206.6 4.7 fusion.94
  212.8 19.0 %all-gather.2 = f32[64,64,2,16]{1,3,2,0:T(8,128)S(1)} all-gather(f32[4,64,2,16]{1,3,2,0:T(8,128)} %copy-done.8), channel_id=4, replica_groups=mesh['slot'=16,'head'=2,'conv'=4] {'slot'}, dimensions={0}, use_global_device_ids=true | all-gather | bytes 557056 | tf_op jit(solution)/shard_map/all_gather | solution.py:83
  232.0 53.3 %while.57 = (s32[]{:T(128)}, f32[1024,2,128]{0,2,1:T(8,128)S(1)}, f32[1024,2,128]{0,2,1:T(8,128)}, f32[4,64,2,16,128]{4,3,2,1,0:T(8,128)}, bf16[4,64,2,16,128]{4...) while((s32[]{:T(128)}, f32[1024,2,128]{0,2,1:T(8,128)S(1)}, ...), condition=%wide.region_11.12_spmd.clone, body=%wide.region_10.11_spmd.clone.sunk | while | flops 2711093248 | bytes 68272416 | solution.py:110
  237.3 3.5 fusion.106
  250.6 3.5 fusion.106
  264.0 3.5 fusion.106
  277.3 3.5 fusion.106
  289.4 73.8 %all-reduce.6.cloned.1.call-done = (f32[1,1024,2,128]{3,2,1,0:T(2,128)}, f32[1,1024,2,128]{3,2,1,0:T(2,128)}) async-done(((f32[1,1024,2,128]{3,2,1,0:T(2,128)}, f32[1,1024,2,128]{3,2,1,0:T(2,128)}), (f32[1,1024,2,128]{3,2,1,0:T(2,128)}, f32[1,1024,2,128]{3,2,1,0:T(2,128)})) %all-reduce.6.cloned.1.call-update) | async-done | bytes 2097168 | tf_op jit(solution)/shard_map/psum | solution.py:119
  365.9 9.8 %divide_subtract_fusion = (f32[2,1024,2,128]{3,2,1,0:T(2,128)}, f32[2,1024,2,128]{3,2,1,0:T(2,128)}, f32[2,1024,2,128]{3,2,1,0:T(2,128)}) fusion(f32[2,1024,2,128]{3,2,1,0:T(2,128)} %param.19, f32[2,1024,2,128]{3,2,1,0:T(2,128)S(1)} %constant_dynamic-update-slice_fusion.3, f32[2,1024,2,128]{3,2,1,0:T(2,128)} %param.20, f32[2,1024,2,128]{3,2,1,0:T(2,128)} %param.21), kind=kLoop, calls=%fused_computation.80 | loop fusion | flops 6291456 | bytes 14680064 | tf_op jit(solution)/shard_map/sub | solution.py:125
  375.7 93.1 %all-reduce.4.cloned.1.call-done = f32[256,32,128]{2,1,0:T(8,128)} async-done(((f32[256,32,128]{2,1,0:T(8,128)}), f32[256,32,128]{2,1,0:T(8,128)}) %all-reduce.4.cloned.1.call-update) | async-done | bytes 4194320 | tf_op jit(solution)/shard_map/psum | solution.py:116
  (164 shorter events, 97.1 us)
Async XLA Ops:
  7.2 49.7 %all-gather.6.cloned.1.call-start = ((), (), s32[]{:S(2)}) async-start(), calls=%async_computation | async-start | bytes 2228224 | tf_op jit(solution)/shard_map/all_gather | solution.py:35
  7.9 95.4 %all-gather.8.cloned.1.call-start = ((), (), s32[]{:S(2)}) async-start(), calls=%async_computation.1 | async-start | bytes 2228224 | tf_op jit(solution)/shard_map/all_gather | solution.py:36
  8.6 354.6 %all-reduce.6.cloned.1.call-start = ((), (), s32[]{:S(2)}) async-start(), calls=%async_computation.3 | async-start | bytes 4194304 | tf_op jit(solution)/shard_map/psum | solution.py:119
  129.8 0.6 copy-start.6
  167.6 1.0 copy-start.1
  211.4 0.8 copy-start.4
  212.2 0.6 copy-start.8
  232.1 2.5 copy-start
  232.1 2.5 copy-start.2
  234.6 2.7 copy-start.5
  237.3 3.5 copy-start.3
  245.4 2.5 copy-start
  245.4 2.5 copy-start.2
  247.9 2.7 copy-start.5
  250.6 3.5 copy-start.3
  258.8 2.5 copy-start
  258.8 2.5 copy-start.2
  261.3 2.7 copy-start.5
  264.0 3.5 copy-start.3
  272.1 2.5 copy-start
  272.1 2.5 copy-start.2
  274.6 2.7 copy-start.5
  277.3 3.5 copy-start.3
  288.9 180.0 %all-reduce.4.cloned.1.call-start = ((), (), s32[]{:S(2)}) async-start(), calls=%async_computation.2 | async-start | bytes 8388608 | tf_op jit(solution)/shard_map/psum | solution.py:116
  (1 other events, 0.6 us)
Sparse Core Ops, SparseCore 0:
  10.1 46.6 all-gather.5
  59.0 44.2 all-gather.7
  289.0 74.2 all-reduce.5
  366.5 102.2 all-reduce.3
